TPU v7x, 512 devices: a whole 4x4x16 slice. The times are simulated.
512 devices in a mesh: user: 32 (over x, y, core), item: 16 (over z).
Axes of the slice: x: 4, y: 4, z: 16, core: 2. Of those that a mesh axis runs over, the one named last changes fastest.
Arguments:
- tokens: bfloat16 [262144, 1024], P(('user', 'item')), may hold values from -6 to 6
- lengths: int32 [512, 32], P(('user', 'item')), may hold values from 1 to 16, as said below
- destination: int32 [512, 32], P(('user', 'item')), may hold values from 0 to 31, as said below
- worker_offset: int32 [512, 32], P(('user', 'item')), may hold values from 0 to 255
- positives: int32 [262144], P(('user', 'item')), may hold values from 0 to 4095, as said below
- negatives: int32 [16, 256], replicated, may hold values from 0 to 4095, as said below
- table: bfloat16 [4096, 1024], P('item'), may hold values from -6 to 6
- in_gain: float32 [1024], replicated, may hold values from 0.1 to 1.9
- w_uvqk: bfloat16 [1024, 2048], P('item'), may hold values from -0.1875 to 0.1875
- out_gain: float32 [512], replicated, may hold values from 0.1 to 1.9
- w_out: bfloat16 [512, 1024], P(None, 'item'), may hold values from -0.25 to 0.25
Outputs:
- layer_out: bfloat16 [131072, 1024], P(('user', 'item'))
- token_grad: bfloat16 [262144, 1024], P(('user', 'item'))
- item_grad: float32 [4096, 1024], P('item', 'user')
Inputs may be any that keep to these rules, and one draw needn't show every extreme that they name: `lengths`: A device's histories lie in its rows in order from row 0 and fill at most 512 rows; every destination receives a history of exactly 16 tokens. `destination`: A device sends its 32 histories to 32 different destinations along user; the histories sent to one device by the devices of its item index, placed at their worker_offset, cover its 256 rows exactly once. `positives`: the target ids of a device lie among the 256 table rows of its item index. `negatives`: columns k * 16 to k * 16 + 15 of each group name rows held by item index k.
All inputs are finite; a program needn't handle non-finite values.
Results may differ from a plain program's by a relative error of at most 0.017.
Values may be sent and summed in bfloat16 or wider, within the bound.
No kernel may reach another device: no remote copies, remote signals or barrier semaphores. Data moves between devices by JAX's collectives and lax.ppermute only.
A program may use at most 64 MiB of HBM per device.

v0:
```python
import jax
import jax.numpy as jnp
from jax import lax
from jax.sharding import PartitionSpec as P

HEAD = 128
TOK_DEV = 256
norm_epsilon = 1e-05
scale_epsilon = 1e-06
inverse_temp = 20.0
loss_scale = 32.0


def joined_along(blocks, dim):
    blocks = jnp.moveaxis(blocks, 0, dim)
    shape = blocks.shape
    return blocks.reshape(*shape[:dim], shape[dim] * shape[dim + 1], *shape[dim + 2 :])


def from_everyone(shard, axis):
    count = lax.axis_size(axis)
    return lax.all_to_all(
        jnp.broadcast_to(shard[None], (count, *shard.shape)), axis, 0, 0, tiled=True
    )


def gather_directly(shard, axis, dim):
    return joined_along(from_everyone(shard, axis), dim)


def in_blocks(shard, dim, count):
    shape = shard.shape
    blocks = shard.reshape(*shape[:dim], count, shape[dim] // count, *shape[dim + 1 :])
    return jnp.moveaxis(blocks, dim, 0)


def sent_and_summed(shard, axis, dim):
    count = lax.axis_size(axis)
    blocks = lax.all_to_all(in_blocks(shard, dim, count), axis, 0, 0, tiled=True)
    return jnp.sum(blocks.astype(jnp.float32), axis=0)


def over_copies(shard, axis):
    everything = from_everyone(shard, axis)
    return jnp.sum(everything, axis=0)


def layer_norm(values, gain):
    center = jnp.mean(values, axis=-1, keepdims=True)
    shifted = values - center
    spread = jnp.mean(shifted * shifted, axis=-1, keepdims=True)
    return shifted * lax.rsqrt(spread + norm_epsilon) * gain


def hstu_block(rows, segment, in_gain, w_uvqk, out_gain, w_out):
    count = rows.shape[0]
    rows_f = rows.astype(jnp.float32)
    normed = layer_norm(rows_f, in_gain).astype(jnp.bfloat16)
    projected = jnp.dot(
        normed,
        lax.all_gather(w_uvqk, "item", axis=0, tiled=True),
        preferred_element_type=jnp.float32,
    )
    active = jax.nn.silu(projected).astype(jnp.bfloat16)
    width = active.shape[1] // 4
    heads = width // HEAD
    gate_u = active[:, :width]
    values_v = active[:, width : 2 * width].reshape(count, heads, HEAD)
    queries = active[:, 2 * width : 3 * width].reshape(count, heads, HEAD)
    key_rows = active[:, 3 * width :].reshape(count, heads, HEAD)
    scores = jnp.einsum(
        "qhd,khd->hqk", queries, key_rows, preferred_element_type=jnp.float32
    ) * HEAD ** (-0.5)
    order = jnp.arange(count, dtype=jnp.int32)
    allowed = (segment[:, None] == segment[None, :]) & (order[None, :] <= order[:, None])
    weights = jnp.where(allowed[None], jax.nn.silu(scores), 0.0).astype(jnp.bfloat16)
    mixed = jnp.einsum(
        "hqk,khd->qhd", weights, values_v, preferred_element_type=jnp.float32
    ).reshape(count, width)
    gated = (layer_norm(mixed, out_gain) * gate_u.astype(jnp.float32)).astype(jnp.bfloat16)
    delta = jnp.dot(gated, gather_directly(w_out, "item", 1), preferred_element_type=jnp.float32)
    return (rows_f + delta).astype(jnp.bfloat16)


def dispatch(rows, home_start, history_len, targets, offsets, slot_rows, user_count):
    peers = jnp.arange(user_count, dtype=jnp.int32)
    chosen = (targets[None, :] == peers[:, None]).astype(jnp.int32)
    first_row = jnp.sum(chosen * home_start[None, :], axis=1)
    sent_count = jnp.sum(chosen * history_len[None, :], axis=1)
    landing = jnp.sum(chosen * offsets[None, :], axis=1)
    within = jnp.arange(slot_rows, dtype=jnp.int32)
    picked = jnp.minimum(first_row[:, None] + within[None, :], rows.shape[0] - 1)
    filled = within[None, :] < sent_count[:, None]
    parcels = jnp.where(filled[:, :, None], rows[picked], jnp.zeros((), rows.dtype))
    labels = jnp.stack([landing, sent_count], axis=1)
    arrived, arrived_labels = (
        lax.all_to_all(parcels, "user", split_axis=0, concat_axis=0, tiled=True),
        lax.all_to_all(labels, "user", split_axis=0, concat_axis=0, tiled=True),
    )
    worker_rows = jnp.arange(TOK_DEV, dtype=jnp.int32)
    lower = arrived_labels[:, 0]
    upper = lower + arrived_labels[:, 1]
    inside = (
        (worker_rows[:, None] >= lower[None, :]) & (worker_rows[:, None] < upper[None, :])
    ).astype(jnp.int32)
    source = jnp.sum(inside * peers[None, :], axis=1)
    begin = jnp.sum(inside * lower[None, :], axis=1)
    flattened = arrived.reshape(-1, arrived.shape[-1])
    gathered = flattened[source * slot_rows + worker_rows - begin]
    return (gathered, source, arrived_labels)


def per_device(
    tokens,
    lengths,
    destination,
    worker_offset,
    positives,
    negatives,
    table,
    in_gain,
    w_uvqk,
    out_gain,
    w_out,
):
    user_count = lax.axis_size("user")
    item_count = lax.axis_size("item")
    item_here = lax.axis_index("item")
    user_here = lax.axis_index("user")
    home_rows = tokens.shape[0]
    model_width = tokens.shape[1]
    hist_count = lengths.shape[1]
    slot_rows = home_rows // hist_count
    history_len = lengths[0]
    targets = destination[0]
    offsets = worker_offset[0]
    home_start = jnp.cumsum(history_len) - history_len
    row_ids = jnp.arange(home_rows, dtype=jnp.int32)
    finished = (row_ids[:, None] >= (home_start + history_len)[None, :]).astype(jnp.int32)
    home_segment = jnp.sum(finished, axis=1)
    valid = row_ids < jnp.sum(history_len)
    home_out = hstu_block(tokens, home_segment, in_gain, w_uvqk, out_gain, w_out)
    layer_out = dispatch(
        home_out, home_start, history_len, targets, offsets, slot_rows, user_count
    )[0]
    item_rows = table.shape[0]
    table_f = table.astype(jnp.float32)
    table_scale = lax.rsqrt(jnp.mean(table_f * table_f, axis=1) + scale_epsilon)
    table_hat = table_f * table_scale[:, None]
    table_low = table_hat.astype(jnp.bfloat16)
    share = negatives.shape[1] // item_count
    owned_ids = (
        lax.dynamic_slice_in_dim(negatives, item_here * share, share, 1) - item_here * item_rows
    )
    group_rows = lax.all_to_all(
        table_low[owned_ids], "item", split_axis=0, concat_axis=0, tiled=True
    ).reshape(-1, model_width)
    positive_local = positives - item_here * item_rows
    positive_rows = table_low[positive_local]
    out_f = home_out.astype(jnp.float32)
    out_scale = lax.rsqrt(jnp.mean(out_f * out_f, axis=1) + scale_epsilon)
    out_hat = out_f * out_scale[:, None]
    out_low = out_hat.astype(jnp.bfloat16)
    factor = inverse_temp / model_width
    positive_logit = (
        jnp.einsum("rd,rd->r", out_low, positive_rows, preferred_element_type=jnp.float32) * factor
    )
    negative_logit = (
        jnp.einsum("rd,nd->rn", out_low, group_rows, preferred_element_type=jnp.float32) * factor
    )
    positive_exp = jnp.exp(positive_logit)
    negative_exp = jnp.exp(negative_logit)
    partition = positive_exp + jnp.sum(negative_exp, axis=1)
    weight = jnp.where(valid, loss_scale, 0.0)
    positive_grad = weight * (positive_exp / partition - 1.0)
    negative_grad = (weight[:, None] * negative_exp / partition[:, None]).astype(jnp.bfloat16)
    grad_hat = (
        positive_grad[:, None] * positive_rows.astype(jnp.float32)
        + jnp.dot(negative_grad, group_rows, preferred_element_type=jnp.float32)
    ) * factor
    token_grad = (
        (grad_hat - out_hat * jnp.mean(grad_hat * out_hat, axis=1, keepdims=True))
        * out_scale[:, None]
    ).astype(jnp.bfloat16)
    negative_terms = (
        jnp.einsum("rn,rd->nd", negative_grad, out_low, preferred_element_type=jnp.float32) * factor
    )
    owned_terms = lax.all_to_all(
        negative_terms.reshape(item_count, share, model_width).astype(jnp.bfloat16),
        "item",
        split_axis=0,
        concat_axis=0,
        tiled=True,
    ).astype(jnp.float32)
    positive_terms = (positive_grad * factor)[:, None] * out_low.astype(jnp.float32)
    catalog = jnp.arange(item_rows, dtype=jnp.int32)
    positive_hits = (positive_local[None, :] == catalog[:, None]).astype(jnp.float32)
    negative_hits = (owned_ids.reshape(-1)[None, :] == catalog[:, None]).astype(jnp.float32)
    row_sums = jnp.dot(positive_hits, positive_terms)
    row_sums = row_sums + jnp.dot(negative_hits, owned_terms.reshape(-1, model_width))
    column_width = model_width // user_count
    part = sent_and_summed(row_sums.astype(jnp.bfloat16), "user", 1)
    hat_part = lax.dynamic_slice_in_dim(table_hat, user_here * column_width, column_width, 1)
    inner = over_copies(jnp.sum(part * hat_part, axis=1), "user") / model_width
    item_grad = (part - hat_part * inner[:, None]) * table_scale[:, None]
    return (layer_out, token_grad, item_grad)


def solution(mesh):
    return jax.shard_map(
        per_device,
        mesh=mesh,
        in_specs=(
            P(("user", "item"), None),
            P(("user", "item"), None),
            P(("user", "item"), None),
            P(("user", "item"), None),
            P(("user", "item")),
            P(),
            P("item", None),
            P(),
            P("item", None),
            P(),
            P(None, "item"),
        ),
        out_specs=(P(("user", "item"), None), P(("user", "item"), None), P("item", "user")),
        check_vma=False,
    )
```

profile of v0, /device:TPU:1, one launch (start us, length us, event | category | flops | bytes accessed | tf_op | source)
XLA Modules:
  0.0 277.3 jit_solution(9776412261107728501)
XLA Ops:
  7.3 0.7 all-gather.2.cloned.1.call-update
  7.9 1.9 broadcast_in_dim.43
  9.9 15.8 %all-to-all-start = ((bf16[16,512,64]{1,2,0:T(8,128)(2,1)}), bf16[16,512,64]{1,2,0:T(8,128)(2,1)}, u32[]{:S(2)}, u32[]{:S(2)}) async-start(bf16[16,512,64]{1,2,0:T(8,128)(2,1)} %broadcast_in_dim.43), calls=%async_computation | async-start | bytes 2097152 | tf_op jit(solution)/shard_map/all_to_all | solution.py:22
  25.7 0.1 copy.50
  25.8 0.1 reduce.6
  25.9 0.1 compare_select_fusion.1
  26.0 0.1 reshape.292
  26.1 0.2 fusion.23
  26.3 1.2 convert_multiply_fusion.8
  27.5 2.0 gather_fusion.2
  29.6 2.0 gather_fusion.3
  31.6 0.7 fusion.61
  32.3 0.1 select_reduce_fusion.2
  32.4 0.7 copy.55
  33.1 0.7 fusion.51
  33.8 0.1 convert_reduce_fusion.2
  33.9 0.2 convert_reduce_fusion
  34.1 0.4 fusion.5
  34.6 0.2 fusion.34
  34.8 87.9 %all-gather.2.cloned.1.call-done = bf16[1024,2048]{1,0:T(8,128)(2,1)} async-done(((bf16[64,2048]{1,0:T(8,128)(2,1)}), bf16[1024,2048]{1,0:T(8,128)(2,1)}) %all-gather.2.cloned.1.call-update) | async-done | bytes 4194320 | tf_op jit(solution)/shard_map/all_gather | solution.py:61
  122.7 5.1 %multiply_convert_fusion = bf16[512,2048]{1,0:T(8,128)(2,1)S(1)} fusion(bf16[1024,2048]{1,0:T(8,128)(2,1)} %all-gather.2.cloned.1.call-done, bf16[512,1024]{1,0:T(8,128)(2,1)S(1)} %copy-done, f32[1024]{0:T(1024)S(1)} %copy-done.8, f32[512]{0:T(512)S(1)} %add_rsqrt_fusion.2, f32[512]{0:T(512)S(1)} %broadcast_multiply_fusion.3), kind=kOutput, calls=%fused_computation.5 | convolution fusion | flops 2155347968 | bytes 7348224 | tf_op jit(solution)/shard_map/dot_general | solution.py:59
  127.7 1.3 copy-done.2
  129.1 1.2 slice_bitcast_fusion.1
  130.3 1.0 copy.66
  131.3 7.0 %all-to-all-start.3 = ((bf16[16,16,1024]{2,1,0:T(8,128)(2,1)}), bf16[16,16,1024]{2,1,0:T(8,128)(2,1)}, u32[]{:S(2)}, u32[]{:S(2)}) async-start(bf16[16,16,1024]{2,1,0:T(8,128)(2,1)} %bitcast.21), calls=%async_computation.3 | async-start | bytes 1048576 | tf_op jit(solution)/shard_map/all_to_all | solution.py:155
  138.3 3.4 %fusion.62 = (f32[512]{0:T(512)S(1)}, f32[4,128,512]{2,1,0:T(8,128)S(1)}) fusion(bf16[512,4,128]{0,2,1:T(8,128)(2,1)} %bitcast.73, pred[512,512]{1,0:T(8,128)(4,1)S(1)} %fusion.34, bf16[64,4,8,128]{3,2,1,0:T(8,128)(2,1)} %get-tuple-element.30, bf16[64,4,8,128]{3,2,1,0:T(8,128)(2,1)} %get-tuple-element.29), kind=kOutput, calls=%fused_computation.120 | convolution fusion | flops 544472576 | bytes 2885632 | tf_op jit(solution)/shard_map/hqk,khd->qhd/dot_general | solution.py:77
  141.7 1.3 copy.67
  143.0 0.2 fusion.29
  143.2 2.6 fusion.12
  145.8 0.5 fusion.15
  146.3 10.5 %all-to-all-done.3 = bf16[16,16,1024]{2,1,0:T(8,128)(2,1)} async-done(((bf16[16,16,1024]{2,1,0:T(8,128)(2,1)}), bf16[16,16,1024]{2,1,0:T(8,128)(2,1)}, u32[]{:S(2)}, u32[]{:S(2)}) %all-to-all-start.3) | async-done | bytes 524320 | tf_op jit(solution)/shard_map/all_to_all | solution.py:155
  156.8 17.8 %all-to-all-start.2 = ((s32[32,1,2]{2,1,0:T(1,128)}), s32[32,1,2]{2,1,0:T(1,128)S(1)}, u32[]{:S(2)}, u32[]{:S(2)}) async-start(s32[32,1,2]{2,1,0:T(1,128)} %copy.55), calls=%async_computation.2 | async-start | bytes 32768 | tf_op jit(solution)/shard_map/all_to_all | solution.py:98
  174.7 1.6 fusion.67
  176.3 0.7 broadcast_multiply_fusion
  177.0 1.4 fusion.20
  178.4 3.2 %all-to-all-done.2 = s32[32,1,2]{2,1,0:T(1,128)S(1)} async-done(((s32[32,1,2]{2,1,0:T(1,128)}), s32[32,1,2]{2,1,0:T(1,128)S(1)}, u32[]{:S(2)}, u32[]{:S(2)}) %all-to-all-start.2) | async-done | bytes 288 | tf_op jit(solution)/shard_map/all_to_all | solution.py:98
  181.6 6.8 %all-to-all-start.4 = ((bf16[16,16,1024]{2,1,0:T(8,128)(2,1)}), bf16[16,16,1024]{2,1,0:T(8,128)(2,1)S(1)}, u32[]{:S(2)}, u32[]{:S(2)}) async-start(bf16[16,16,1024]{2,1,0:T(8,128)(2,1)} %bitcast.23), calls=%async_computation.4 | async-start | bytes 1048576 | tf_op jit(solution)/shard_map/all_to_all | solution.py:188
  188.4 0.1 eq.70
  188.5 0.1 compare_select_fusion
  188.5 0.1 reshape.268
  188.6 0.1 iota_compare_fusion.9
  188.7 0.1 copy.56
  188.8 22.6 %all-to-all-done.4 = bf16[16,16,1024]{2,1,0:T(8,128)(2,1)S(1)} async-done(((bf16[16,16,1024]{2,1,0:T(8,128)(2,1)}), bf16[16,16,1024]{2,1,0:T(8,128)(2,1)S(1)}, u32[]{:S(2)}, u32[]{:S(2)}) %all-to-all-start.4) | async-done | bytes 524320 | tf_op jit(solution)/shard_map/all_to_all | solution.py:188
  211.4 0.3 fusion.48
  211.7 0.6 fusion.21
  212.3 1.0 copy.57
  213.3 11.2 %all-to-all-start.5 = ((bf16[32,256,32]{1,2,0:T(8,128)(2,1)}), bf16[32,256,32]{1,2,0:T(8,128)(2,1)}, u32[]{:S(2)}, u32[]{:S(2)}) async-start(bf16[32,256,32]{1,2,0:T(8,128)(2,1)} %bitcast.26), calls=%async_computation.5 | async-start | bytes 1048576 | tf_op jit(solution)/shard_map/all_to_all | solution.py:39
  224.6 0.1 select_reduce_fusion.1
  224.7 2.1 gather_fusion
  226.7 1.1 broadcast_select_fusion
  227.8 8.5 %all-to-all-done.5 = bf16[32,256,32]{1,2,0:T(8,128)(2,1)} async-done(((bf16[32,256,32]{1,2,0:T(8,128)(2,1)}), bf16[32,256,32]{1,2,0:T(8,128)(2,1)}, u32[]{:S(2)}, u32[]{:S(2)}) %all-to-all-start.5) | async-done | bytes 524320 | tf_op jit(solution)/shard_map/all_to_all | solution.py:39
  236.3 3.7 %all-to-all-start.1 = ((bf16[32,16,1024]{2,1,0:T(8,128)(2,1)}), bf16[32,16,1024]{2,1,0:T(8,128)(2,1)S(1)}, u32[]{:S(2)}, u32[]{:S(2)}) async-start(bf16[32,16,1024]{2,1,0:T(8,128)(2,1)} %broadcast_select_fusion), calls=%async_computation.1 | async-start | bytes 2097152 | tf_op jit(solution)/shard_map/all_to_all | solution.py:97
  240.1 3.3 %fusion.8 = (f32[512]{0:T(512)S(1)}, f32[512,1024]{1,0:T(8,128)}) fusion(bf16[512,1024]{1,0:T(8,128)(2,1)S(1)} %get-tuple-element.40, f32[512]{0:T(512)S(1)} %add_rsqrt_fusion, bf16[256,1024]{1,0:T(8,128)(2,1)} %bitcast.22, f32[512,256]{0,1:T(8,128)} %copy-done.10, f32[512]{0:T(512)S(1)} %get-tuple-element.34, f32[512]{0:T(512)S(1)} %fusion.51, ...), kind=kOutput, calls=%fused_computation.22 | convolution fusion | flops 273022464 | bytes 5253120 | tf_op jit(solution)/shard_map/dot_general | solution.py:179
  243.4 1.1 convert_reduce_fusion.1
  244.5 0.1 copy.60
  244.6 1.1 multiply_reduce_fusion
  245.7 11.1 %all-to-all-done.1 = bf16[32,16,1024]{2,1,0:T(8,128)(2,1)S(1)} async-done(((bf16[32,16,1024]{2,1,0:T(8,128)(2,1)}), bf16[32,16,1024]{2,1,0:T(8,128)(2,1)S(1)}, u32[]{:S(2)}, u32[]{:S(2)}) %all-to-all-start.1) | async-done | bytes 1048608 | tf_op jit(solution)/shard_map/all_to_all | solution.py:97
  256.8 0.6 broadcast_in_dim.50
  257.4 3.9 %all-to-all-start.6 = ((f32[32,1,256]{2,1,0:T(1,128)}), f32[32,1,256]{2,1,0:T(1,128)S(1)}, u32[]{:S(2)}, u32[]{:S(2)}) async-start(f32[32,1,256]{2,1,0:T(1,128)} %broadcast_in_dim.50), calls=%async_computation.6 | async-start | bytes 65536 | tf_op jit(solution)/shard_map/all_to_all | solution.py:22
  261.4 3.0 %fusion.11 = bf16[512,1024]{1,0:T(8,128)(2,1)} fusion(f32[512,1024]{1,0:T(8,128)} %get-tuple-element.44, bf16[512,1024]{1,0:T(8,128)(2,1)S(1)} %get-tuple-element.40, f32[512]{0:T(512)S(1)} %broadcast_multiply_fusion.2, f32[512]{0:T(512)S(1)} %add_rsqrt_fusion), kind=kLoop, calls=%fused_computation.25 | loop fusion | flops 3145728 | bytes 4198400 | tf_op jit(solution)/shard_map/convert_element_type | solution.py:184
  264.4 2.0 gather_fusion.1
  266.3 2.3 all-to-all-done.6
  268.7 1.1 subtract_multiply_fusion
  269.8 0.7 copy.61
  (43 shorter events, 0.3 us)
Async XLA Ops:
  7.2 18.5 %copy-start.3 = (s32[1,32]{1,0:T(1,128)S(1)}, s32[1,32]{1,0:T(1,128)}, u32[]{:S(2)}) copy-start(s32[1,32]{1,0:T(1,128)} %param.12) | copy-start | bytes 388
  7.2 18.7 %copy-start.4 = (s32[16,256]{1,0:T(8,128)S(1)}, s32[16,256]{1,0:T(8,128)}, u32[]{:S(2)}) copy-start(s32[16,256]{1,0:T(8,128)} %param.16) | copy-start | bytes 49156
  7.2 18.9 %copy-start.5 = (s32[512]{0:T(512)S(1)}, s32[512]{0:T(512)}, u32[]{:S(2)}) copy-start(s32[512]{0:T(512)} %param.15) | copy-start | bytes 6148
  7.2 18.9 %copy-start.1 = (bf16[256,1024]{1,0:T(8,128)(2,1)S(1)}, bf16[256,1024]{1,0:T(8,128)(2,1)}, u32[]{:S(2)}) copy-start(bf16[256,1024]{1,0:T(8,128)(2,1)} %param.17) | copy-start | bytes 1572868
  7.2 115.4 %all-gather.2.cloned.1.call-start = ((), (), s32[]{:S(2)}) async-start(), calls=%async_computation.7 | async-start | bytes 4456448 | tf_op jit(solution)/shard_map/all_gather | solution.py:61
  9.9 121.4 %all-to-all-start = ((bf16[16,512,64]{1,2,0:T(8,128)(2,1)}), bf16[16,512,64]{1,2,0:T(8,128)(2,1)}, u32[]{:S(2)}, u32[]{:S(2)}) async-start(bf16[16,512,64]{1,2,0:T(8,128)(2,1)} %broadcast_in_dim.43), calls=%async_computation | async-start | bytes 2097152 | tf_op jit(solution)/shard_map/all_to_all | solution.py:22
  29.5 2.7 copy-start.6
  29.6 2.7 copy-start.7
  29.6 4.4 %copy-start = (bf16[512,1024]{1,0:T(8,128)(2,1)S(1)}, bf16[512,1024]{1,0:T(8,128)(2,1)}, u32[]{:S(2)}) copy-start(bf16[512,1024]{1,0:T(8,128)(2,1)} %param.11) | copy-start | bytes 3145732
  31.6 91.1 %copy-start.8 = (f32[1024]{0:T(1024)S(1)}, f32[1024]{0:T(1024)}, u32[]{:S(2)}) copy-start(f32[1024]{0:T(1024)} %param.18) | copy-start | bytes 12292
  127.7 1.4 copy-start.2
  131.3 25.5 %all-to-all-start.3 = ((bf16[16,16,1024]{2,1,0:T(8,128)(2,1)}), bf16[16,16,1024]{2,1,0:T(8,128)(2,1)}, u32[]{:S(2)}, u32[]{:S(2)}) async-start(bf16[16,16,1024]{2,1,0:T(8,128)(2,1)} %bitcast.21), calls=%async_computation.3 | async-start | bytes 1048576 | tf_op jit(solution)/shard_map/all_to_all | solution.py:155
  141.7 1.5 copy-start.9
  156.8 24.8 %all-to-all-start.2 = ((s32[32,1,2]{2,1,0:T(1,128)}), s32[32,1,2]{2,1,0:T(1,128)S(1)}, u32[]{:S(2)}, u32[]{:S(2)}) async-start(s32[32,1,2]{2,1,0:T(1,128)} %copy.55), calls=%async_computation.2 | async-start | bytes 32768 | tf_op jit(solution)/shard_map/all_to_all | solution.py:98
  176.3 5.3 %copy-start.10 = (f32[512,256]{0,1:T(8,128)}, f32[512,256]{0,1:T(8,128)S(1)}, u32[]{:S(2)}) copy-start(f32[512,256]{0,1:T(8,128)S(1)} %get-tuple-element.42) | copy-start | bytes 1572868
  181.6 29.8 %all-to-all-start.4 = ((bf16[16,16,1024]{2,1,0:T(8,128)(2,1)}), bf16[16,16,1024]{2,1,0:T(8,128)(2,1)S(1)}, u32[]{:S(2)}, u32[]{:S(2)}) async-start(bf16[16,16,1024]{2,1,0:T(8,128)(2,1)} %bitcast.23), calls=%async_computation.4 | async-start | bytes 1048576 | tf_op jit(solution)/shard_map/all_to_all | solution.py:188
  213.3 23.0 %all-to-all-start.5 = ((bf16[32,256,32]{1,2,0:T(8,128)(2,1)}), bf16[32,256,32]{1,2,0:T(8,128)(2,1)}, u32[]{:S(2)}, u32[]{:S(2)}) async-start(bf16[32,256,32]{1,2,0:T(8,128)(2,1)} %bitcast.26), calls=%async_computation.5 | async-start | bytes 1048576 | tf_op jit(solution)/shard_map/all_to_all | solution.py:39
  236.3 20.5 %all-to-all-start.1 = ((bf16[32,16,1024]{2,1,0:T(8,128)(2,1)}), bf16[32,16,1024]{2,1,0:T(8,128)(2,1)S(1)}, u32[]{:S(2)}, u32[]{:S(2)}) async-start(bf16[32,16,1024]{2,1,0:T(8,128)(2,1)} %broadcast_select_fusion), calls=%async_computation.1 | async-start | bytes 2097152 | tf_op jit(solution)/shard_map/all_to_all | solution.py:97
  257.4 11.2 %all-to-all-start.6 = ((f32[32,1,256]{2,1,0:T(1,128)}), f32[32,1,256]{2,1,0:T(1,128)S(1)}, u32[]{:S(2)}, u32[]{:S(2)}) async-start(f32[32,1,256]{2,1,0:T(1,128)} %broadcast_in_dim.50), calls=%async_computation.6 | async-start | bytes 65536 | tf_op jit(solution)/shard_map/all_to_all | solution.py:22
Sparse Core Ops, SparseCore 0:
  10.1 112.5 all-gather.1
where the time goes:
time: 278 us; the launch traced here: 277 us
  waiting for transfers between devices  147 us (53%)
  starting transfers between devices  66.3 us (24%)
  local copies, waits for them, and re-layouts  18.4 us (7%)
  matrix products  18.3 us (7%)
  between operations  14.4 us (5%)
  other arithmetic  13.3 us (5%)
    all_gather x1, waiting for transfers between devices, hstu_block(): lax.all_gather(w_uvqk, 'item', axis=0, tiled=True)  87.9 us
    all_to_all x1, waiting for transfers between devices, per_device(): lax.all_to_all(negative_terms.reshape(item_count, share, model_width).ast...  22.6 us
    all_to_all x2, starting transfers between devices, from_everyone(): lax.all_to_all(jnp.broadcast_to(shard[None], (count, *shard.shape)), axis...  19.7 us
    all_to_all x1, starting transfers between devices, dispatch(): lax.all_to_all(labels, 'user', split_axis=0, concat_axis=0, tiled=True)  17.8 us
    all_to_all x1, starting transfers between devices, sent_and_summed(): lax.all_to_all(in_blocks(shard, dim, count), axis, 0, 0, tiled=True)  11.2 us
    all_to_all x1, waiting for transfers between devices, dispatch(): lax.all_to_all(parcels, 'user', split_axis=0, concat_axis=0, tiled=True)  11.1 us
    all_to_all x1, waiting for transfers between devices, per_device(): lax.all_to_all(table_low[owned_ids], 'item', split_axis=0, concat_axis=0,...  10.5 us
    all_to_all x1, waiting for transfers between devices, sent_and_summed(): lax.all_to_all(in_blocks(shard, dim, count), axis, 0, 0, tiled=True)  8.47 us
  transfers between devices with their start and end apart: 8, of which 7 were waited for; matrix products, arithmetic and copies ran while one was open for 16% of the time, Pallas kernels for 0%

commit v1 on v0

--- a/solution.py
+++ b/solution.py
@@ -11,6 +11,24 @@
 loss_scale = 32.0
 
 
+def gather_around(array, axis, dim):
+    ways, here, hop = (lax.axis_size(axis), lax.axis_index(axis), array.shape[dim])
+    shape = [n * ways if d == dim else n for d, n in enumerate(array.shape)]
+    full = lax.dynamic_update_slice_in_dim(
+        jnp.zeros(shape, array.dtype), array, here * hop, axis=dim
+    )
+    going_up = going_down = array
+    for far in range(1, ways // 2 + 1):
+        going_up = lax.ppermute(going_up, axis, [(d, (d + 1) % ways) for d in range(ways)])
+        full = lax.dynamic_update_slice_in_dim(full, going_up, (here - far) % ways * hop, axis=dim)
+        if 2 * far < ways:
+            going_down = lax.ppermute(going_down, axis, [(d, (d - 1) % ways) for d in range(ways)])
+            full = lax.dynamic_update_slice_in_dim(
+                full, going_down, (here + far) % ways * hop, axis=dim
+            )
+    return full
+
+
 def joined_along(blocks, dim):
     blocks = jnp.moveaxis(blocks, 0, dim)
     shape = blocks.shape
@@ -57,9 +75,7 @@
     rows_f = rows.astype(jnp.float32)
     normed = layer_norm(rows_f, in_gain).astype(jnp.bfloat16)
     projected = jnp.dot(
-        normed,
-        lax.all_gather(w_uvqk, "item", axis=0, tiled=True),
-        preferred_element_type=jnp.float32,
+        normed, gather_around(w_uvqk, "item", 0), preferred_element_type=jnp.float32
     )
     active = jax.nn.silu(projected).astype(jnp.bfloat16)
     width = active.shape[1] // 4

time: 278 us -> 287 us (1.032)
  starting transfers between devices: 66.3 us -> 118 us
  waiting for transfers between devices: 147 us -> 96.1 us
  local copies, waits for them, and re-layouts: 18.4 us -> 35.1 us
  between operations: 14.4 us -> 1.38 us
    all_gather x1 -> x0, waiting for transfers between devices: 87.9 us -> none  [hstu_block(): lax.all_gather(w_uvqk, 'item', axis=0, tiled=True)]
    ppermute x0 -> x15, starting transfers between devices: none -> 54.8 us  [the longest x7 35.6 us: gather_around(): lax.ppermute(going_down, axis, [(d, (d - 1) % ways) for d in range(ways)])]
    ppermute x0 -> x15, waiting for transfers between devices: none -> 37.4 us  [the longest x8 37.4 us: gather_around(): lax.ppermute(going_up, axis, [(d, (d + 1) % ways) for d in range(ways)])]
    dynamic_update_slice x0 -> x16, local copies, waits for them, and re-layouts: none -> 13.5 us  [the longest x8 6.81 us: gather_around(): lax.dynamic_update_slice_in_dim(full, going_up, (here - far) % ways * hop...]
    all_to_all x2, starting transfers between devices: 19.7 us -> 12.3 us  [from_everyone(): lax.all_to_all(jnp.broadcast_to(shard[None], (count, *shard.shape)), axis...]
    all_to_all x1, starting transfers between devices: 6.96 us -> 11.9 us  [per_device(): lax.all_to_all(table_low[owned_ids], 'item', split_axis=0, concat_axis=0,...]
  transfers between devices with their start and end apart: 8 -> 22, of which waited for: 7 -> 13; matrix products, arithmetic and copies ran while one was open for 16% -> 23% of each run, Pallas kernels for 0% -> 0%
where the time goes in v1:
time: 287 us; the launch traced here: 285 us
  starting transfers between devices  118 us (41%)
  waiting for transfers between devices  96.1 us (33%)
  local copies, waits for them, and re-layouts  35.1 us (12%)
  matrix products  19.7 us (7%)
  other arithmetic  15 us (5%)
    ppermute x8, waiting for transfers between devices, gather_around(): lax.ppermute(going_up, axis, [(d, (d + 1) % ways) for d in range(ways)])  37.4 us
    ppermute x7, starting transfers between devices, gather_around(): lax.ppermute(going_down, axis, [(d, (d - 1) % ways) for d in range(ways)])  35.6 us
    all_to_all x1, waiting for transfers between devices, per_device(): lax.all_to_all(negative_terms.reshape(item_count, share, model_width).ast...  22.6 us
    ppermute x8, starting transfers between devices, gather_around(): lax.ppermute(going_up, axis, [(d, (d + 1) % ways) for d in range(ways)])  19.2 us
    all_to_all x1, starting transfers between devices, dispatch(): lax.all_to_all(labels, 'user', split_axis=0, concat_axis=0, tiled=True)  17.2 us
    all_to_all x2, starting transfers between devices, from_everyone(): lax.all_to_all(jnp.broadcast_to(shard[None], (count, *shard.shape)), axis...  12.3 us
    all_to_all x1, starting transfers between devices, per_device(): lax.all_to_all(table_low[owned_ids], 'item', split_axis=0, concat_axis=0,...  11.9 us
    all_to_all x1, starting transfers between devices, sent_and_summed(): lax.all_to_all(in_blocks(shard, dim, count), axis, 0, 0, tiled=True)  11.2 us
  transfers between devices with their start and end apart: 22, of which 13 were waited for; matrix products, arithmetic and copies ran while one was open for 23% of the time, Pallas kernels for 0%

profile of v1, /device:TPU:1, one launch (start us, length us, event | category | flops | bytes accessed | tf_op | source)
XLA Modules:
  0.0 285.4 jit_solution(17931109207435703850)
XLA Ops:
  0.7 4.5 %collective-permute-start = (bf16[64,2048]{1,0:T(8,128)(2,1)}, bf16[64,2048]{1,0:T(8,128)(2,1)}, u32[]{:S(2)}, u32[]{:S(2)}) collective-permute-start(bf16[64,2048]{1,0:T(8,128)(2,1)} %param.19), channel_id=1, source_target_pairs={{0,1},{1,2},{2,3},{3,4},{4,5},{5,6},{6,7},{7,8},{8,9},{9,10},{10,1... | collective-permute-start | bytes 786440 | tf_op jit(solution)/shard_map/ppermute | solution.py:22
  5.2 9.5 %collective-permute-start.1 = (bf16[64,2048]{1,0:T(8,128)(2,1)}, bf16[64,2048]{1,0:T(8,128)(2,1)}, u32[]{:S(2)}, u32[]{:S(2)}) collective-permute-start(bf16[64,2048]{1,0:T(8,128)(2,1)} %param.19), channel_id=1, source_target_pairs={{0,15},{1,0},{2,1},{3,2},{4,3},{5,4},{6,5},{7,6},{8,7},{9,8},{10,9... | collective-permute-start | bytes 786440 | tf_op jit(solution)/shard_map/ppermute | solution.py:25
  14.7 1.9 broadcast_in_dim.46
  16.6 8.4 %all-to-all-start = ((bf16[16,512,64]{1,2,0:T(8,128)(2,1)}), bf16[16,512,64]{1,2,0:T(8,128)(2,1)}, u32[]{:S(2)}, u32[]{:S(2)}) async-start(bf16[16,512,64]{1,2,0:T(8,128)(2,1)} %broadcast_in_dim.46), calls=%async_computation | async-start | bytes 2097152 | tf_op jit(solution)/shard_map/all_to_all | solution.py:40
  25.0 0.7 copy.50
  26.0 1.3 fusion.61
  27.4 1.4 convert_reduce_fusion
  29.5 1.2 convert_multiply_fusion.8
  31.5 2.5 broadcast_in_dim.43
  35.1 2.1 gather_fusion.2
  37.2 2.0 gather_fusion.3
  40.1 3.2 %collective-permute-start.2 = (bf16[64,2048]{1,0:T(8,128)(2,1)}, bf16[64,2048]{1,0:T(8,128)(2,1)S(1)}, u32[]{:S(2)}, u32[]{:S(2)}) collective-permute-start(bf16[64,2048]{1,0:T(8,128)(2,1)} %collective-permute-done), channel_id=1, source_target_pairs={{0,1},{1,2},{2,3},{3,4},{4,5},{5,6},{6,7},{7,8},{8,9},{9,10},{10,1... | collective-permute-start | bytes 786440 | tf_op jit(solution)/shard_map/ppermute | solution.py:22
  43.3 3.3 %collective-permute-start.3 = (bf16[64,2048]{1,0:T(8,128)(2,1)}, bf16[64,2048]{1,0:T(8,128)(2,1)S(1)}, u32[]{:S(2)}, u32[]{:S(2)}) collective-permute-start(bf16[64,2048]{1,0:T(8,128)(2,1)} %collective-permute-done.1), channel_id=1, source_target_pairs={{0,15},{1,0},{2,1},{3,2},{4,3},{5,4},{6,5},{7,6},{8,7},{9,8},{10,9... | collective-permute-start | bytes 786440 | tf_op jit(solution)/shard_map/ppermute | solution.py:25
  46.6 1.7 constant_dynamic-update-slice_fusion.14
  48.3 1.7 constant_dynamic-update-slice_fusion.13
  50.0 28.7 %collective-permute-done.2 = bf16[64,2048]{1,0:T(8,128)(2,1)S(1)} collective-permute-done((bf16[64,2048]{1,0:T(8,128)(2,1)}, bf16[64,2048]{1,0:T(8,128)(2,1)S(1)}, u32[]{:S(2)}, u32[]{:S(2)}) %collective-permute-start.2) | collective-permute-done | bytes 262176 | tf_op jit(solution)/shard_map/ppermute | solution.py:22
  78.6 1.9 collective-permute-start.4
  80.6 4.6 %collective-permute-start.5 = (bf16[64,2048]{1,0:T(8,128)(2,1)S(1)}, bf16[64,2048]{1,0:T(8,128)(2,1)S(1)}, u32[]{:S(2)}, u32[]{:S(2)}) collective-permute-start(bf16[64,2048]{1,0:T(8,128)(2,1)S(1)} %collective-permute-done.3), channel_id=1, source_target_pairs={{0,15},{1,0},{2,1},{3,2},{4,3},{5,4},{6,5},{7,6},{8,7},{9,8},{10,9... | collective-permute-start | bytes 786440 | tf_op jit(solution)/shard_map/ppermute | solution.py:25
  86.6 1.6 collective-permute-done.4
  88.2 1.9 collective-permute-start.6
  90.1 4.6 %collective-permute-start.7 = (bf16[64,2048]{1,0:T(8,128)(2,1)S(1)}, bf16[64,2048]{1,0:T(8,128)(2,1)S(1)}, u32[]{:S(2)}, u32[]{:S(2)}) collective-permute-start(bf16[64,2048]{1,0:T(8,128)(2,1)S(1)} %collective-permute-done.5), channel_id=1, source_target_pairs={{0,15},{1,0},{2,1},{3,2},{4,3},{5,4},{6,5},{7,6},{8,7},{9,8},{10,9... | collective-permute-start | bytes 786440 | tf_op jit(solution)/shard_map/ppermute | solution.py:25
  94.7 0.7 constant_dynamic-update-slice_fusion.10
  96.2 0.7 collective-permute-done.6
  96.9 1.9 collective-permute-start.8
  98.8 4.6 %collective-permute-start.9 = (bf16[64,2048]{1,0:T(8,128)(2,1)S(1)}, bf16[64,2048]{1,0:T(8,128)(2,1)S(1)}, u32[]{:S(2)}, u32[]{:S(2)}) collective-permute-start(bf16[64,2048]{1,0:T(8,128)(2,1)S(1)} %collective-permute-done.7), channel_id=1, source_target_pairs={{0,15},{1,0},{2,1},{3,2},{4,3},{5,4},{6,5},{7,6},{8,7},{9,8},{10,9... | collective-permute-start | bytes 786440 | tf_op jit(solution)/shard_map/ppermute | solution.py:25
  103.4 0.7 constant_dynamic-update-slice_fusion.8
  104.2 0.7 constant_dynamic-update-slice_fusion.7
  105.2 1.9 collective-permute-start.10
  107.2 4.6 %collective-permute-start.11 = (bf16[64,2048]{1,0:T(8,128)(2,1)S(1)}, bf16[64,2048]{1,0:T(8,128)(2,1)S(1)}, u32[]{:S(2)}, u32[]{:S(2)}) collective-permute-start(bf16[64,2048]{1,0:T(8,128)(2,1)S(1)} %collective-permute-done.9), channel_id=1, source_target_pairs={{0,15},{1,0},{2,1},{3,2},{4,3},{5,4},{6,5},{7,6},{8,7},{9,8},{10,9... | collective-permute-start | bytes 786440 | tf_op jit(solution)/shard_map/ppermute | solution.py:25
  111.7 0.7 constant_dynamic-update-slice_fusion.6
  113.6 1.9 collective-permute-start.12
  115.5 4.6 %collective-permute-start.13 = (bf16[64,2048]{1,0:T(8,128)(2,1)S(1)}, bf16[64,2048]{1,0:T(8,128)(2,1)S(1)}, u32[]{:S(2)}, u32[]{:S(2)}) collective-permute-start(bf16[64,2048]{1,0:T(8,128)(2,1)S(1)} %collective-permute-done.11), channel_id=1, source_target_pairs={{0,15},{1,0},{2,1},{3,2},{4,3},{5,4},{6,5},{7,6},{8,7},{9,8},{10,9... | collective-permute-start | bytes 786440 | tf_op jit(solution)/shard_map/ppermute | solution.py:25
  121.9 1.9 collective-permute-start.14
  125.2 5.3 %collective-permute-done.14 = bf16[64,2048]{1,0:T(8,128)(2,1)S(1)} collective-permute-done((bf16[64,2048]{1,0:T(8,128)(2,1)S(1)}, bf16[64,2048]{1,0:T(8,128)(2,1)S(1)}, u32[]{:S(2)}, u32[]{:S(2)}) %collective-permute-start.14) | collective-permute-done | bytes 262176 | tf_op jit(solution)/shard_map/ppermute | solution.py:22
  130.5 0.7 constant_dynamic-update-slice_fusion
  131.3 6.4 %multiply_convert_fusion = bf16[512,2048]{1,0:T(8,128)(2,1)} fusion(bf16[1024,2048]{1,0:T(8,128)(2,1)} %constant_dynamic-update-slice_fusion, bf16[512,1024]{1,0:T(8,128)(2,1)S(1)} %copy-done, f32[1024]{0:T(1024)S(1)} %copy-done.8, f32[512]{0:T(512)S(1)} %add_rsqrt_fusion.2, f32[512]{0:T(512)S(1)} %broadcast_multiply_fusion.3), kind=kOutput, calls=%fused_computation.5 | convolution fusion | flops 2155347968 | bytes 7348224 | tf_op jit(solution)/shard_map/dot_general | solution.py:77
  137.7 2.6 slice_bitcast_fusion.1
  140.3 1.0 copy.66
  141.3 11.9 %all-to-all-start.3 = ((bf16[16,16,1024]{2,1,0:T(8,128)(2,1)}), bf16[16,16,1024]{2,1,0:T(8,128)(2,1)}, u32[]{:S(2)}, u32[]{:S(2)}) async-start(bf16[16,16,1024]{2,1,0:T(8,128)(2,1)} %bitcast.21), calls=%async_computation.3 | async-start | bytes 1048576 | tf_op jit(solution)/shard_map/all_to_all | solution.py:171
  153.2 3.4 %fusion.62 = (f32[512]{0:T(512)S(1)}, f32[4,128,512]{2,1,0:T(8,128)S(1)}) fusion(bf16[512,4,128]{0,2,1:T(8,128)(2,1)} %bitcast.73, pred[512,512]{1,0:T(8,128)(4,1)S(1)} %fusion.34, bf16[64,4,8,128]{3,2,1,0:T(8,128)(2,1)} %get-tuple-element.30, bf16[64,4,8,128]{3,2,1,0:T(8,128)(2,1)} %get-tuple-element.29), kind=kOutput, calls=%fused_computation.136 | convolution fusion | flops 544472576 | bytes 2885632 | tf_op jit(solution)/shard_map/hqk,khd->qhd/dot_general | solution.py:93
  156.6 1.3 copy.67
  158.1 2.6 fusion.12
  161.2 11.0 %all-to-all-done.3 = bf16[16,16,1024]{2,1,0:T(8,128)(2,1)} async-done(((bf16[16,16,1024]{2,1,0:T(8,128)(2,1)}), bf16[16,16,1024]{2,1,0:T(8,128)(2,1)}, u32[]{:S(2)}, u32[]{:S(2)}) %all-to-all-start.3) | async-done | bytes 524320 | tf_op jit(solution)/shard_map/all_to_all | solution.py:171
  172.2 17.2 %all-to-all-start.2 = ((s32[32,1,2]{2,1,0:T(1,128)}), s32[32,1,2]{2,1,0:T(1,128)S(1)}, u32[]{:S(2)}, u32[]{:S(2)}) async-start(s32[32,1,2]{2,1,0:T(1,128)} %copy.55), calls=%async_computation.2 | async-start | bytes 32768 | tf_op jit(solution)/shard_map/all_to_all | solution.py:114
  189.4 1.6 fusion.67
  191.7 1.4 fusion.20
  193.1 3.2 %all-to-all-done.2 = s32[32,1,2]{2,1,0:T(1,128)S(1)} async-done(((s32[32,1,2]{2,1,0:T(1,128)}), s32[32,1,2]{2,1,0:T(1,128)S(1)}, u32[]{:S(2)}, u32[]{:S(2)}) %all-to-all-start.2) | async-done | bytes 288 | tf_op jit(solution)/shard_map/all_to_all | solution.py:114
  196.3 6.9 %all-to-all-start.4 = ((bf16[16,16,1024]{2,1,0:T(8,128)(2,1)}), bf16[16,16,1024]{2,1,0:T(8,128)(2,1)S(1)}, u32[]{:S(2)}, u32[]{:S(2)}) async-start(bf16[16,16,1024]{2,1,0:T(8,128)(2,1)} %bitcast.23), calls=%async_computation.4 | async-start | bytes 1048576 | tf_op jit(solution)/shard_map/all_to_all | solution.py:204
  203.7 22.6 %all-to-all-done.4 = bf16[16,16,1024]{2,1,0:T(8,128)(2,1)S(1)} async-done(((bf16[16,16,1024]{2,1,0:T(8,128)(2,1)}), bf16[16,16,1024]{2,1,0:T(8,128)(2,1)S(1)}, u32[]{:S(2)}, u32[]{:S(2)}) %all-to-all-start.4) | async-done | bytes 524320 | tf_op jit(solution)/shard_map/all_to_all | solution.py:204
  227.2 1.0 copy.57
  228.2 11.2 %all-to-all-start.5 = ((bf16[32,256,32]{1,2,0:T(8,128)(2,1)}), bf16[32,256,32]{1,2,0:T(8,128)(2,1)}, u32[]{:S(2)}, u32[]{:S(2)}) async-start(bf16[32,256,32]{1,2,0:T(8,128)(2,1)} %bitcast.26), calls=%async_computation.5 | async-start | bytes 1048576 | tf_op jit(solution)/shard_map/all_to_all | solution.py:57
  239.5 2.1 gather_fusion
  241.6 1.1 broadcast_select_fusion
  242.7 8.5 %all-to-all-done.5 = bf16[32,256,32]{1,2,0:T(8,128)(2,1)} async-done(((bf16[32,256,32]{1,2,0:T(8,128)(2,1)}), bf16[32,256,32]{1,2,0:T(8,128)(2,1)}, u32[]{:S(2)}, u32[]{:S(2)}) %all-to-all-start.5) | async-done | bytes 524320 | tf_op jit(solution)/shard_map/all_to_all | solution.py:57
  251.2 3.7 %all-to-all-start.1 = ((bf16[32,16,1024]{2,1,0:T(8,128)(2,1)}), bf16[32,16,1024]{2,1,0:T(8,128)(2,1)S(1)}, u32[]{:S(2)}, u32[]{:S(2)}) async-start(bf16[32,16,1024]{2,1,0:T(8,128)(2,1)} %broadcast_select_fusion), calls=%async_computation.1 | async-start | bytes 2097152 | tf_op jit(solution)/shard_map/all_to_all | solution.py:113
  255.0 3.3 %fusion.8 = (f32[512]{0:T(512)S(1)}, f32[512,1024]{1,0:T(8,128)}) fusion(bf16[512,1024]{1,0:T(8,128)(2,1)S(1)} %get-tuple-element.40, f32[512]{0:T(512)S(1)} %add_rsqrt_fusion, bf16[256,1024]{1,0:T(8,128)(2,1)} %bitcast.22, f32[512,256]{0,1:T(8,128)} %copy-done.10, f32[512]{0:T(512)S(1)} %get-tuple-element.34, f32[512]{0:T(512)S(1)} %fusion.51, ...), kind=kOutput, calls=%fused_computation.22 | convolution fusion | flops 273022464 | bytes 5253120 | tf_op jit(solution)/shard_map/dot_general | solution.py:195
  258.3 1.1 convert_reduce_fusion.1
  259.5 1.1 multiply_reduce_fusion
  260.6 11.1 %all-to-all-done.1 = bf16[32,16,1024]{2,1,0:T(8,128)(2,1)S(1)} async-done(((bf16[32,16,1024]{2,1,0:T(8,128)(2,1)}), bf16[32,16,1024]{2,1,0:T(8,128)(2,1)S(1)}, u32[]{:S(2)}, u32[]{:S(2)}) %all-to-all-start.1) | async-done | bytes 1048608 | tf_op jit(solution)/shard_map/all_to_all | solution.py:113
  272.3 3.9 %all-to-all-start.6 = ((f32[32,1,256]{2,1,0:T(1,128)}), f32[32,1,256]{2,1,0:T(1,128)S(1)}, u32[]{:S(2)}, u32[]{:S(2)}) async-start(f32[32,1,256]{2,1,0:T(1,128)} %broadcast_in_dim.55), calls=%async_computation.6 | async-start | bytes 65536 | tf_op jit(solution)/shard_map/all_to_all | solution.py:40
  276.3 3.0 %fusion.11 = bf16[512,1024]{1,0:T(8,128)(2,1)} fusion(f32[512,1024]{1,0:T(8,128)} %get-tuple-element.44, bf16[512,1024]{1,0:T(8,128)(2,1)S(1)} %get-tuple-element.40, f32[512]{0:T(512)S(1)} %broadcast_multiply_fusion.2, f32[512]{0:T(512)S(1)} %add_rsqrt_fusion), kind=kLoop, calls=%fused_computation.25 | loop fusion | flops 3145728 | bytes 4198400 | tf_op jit(solution)/shard_map/convert_element_type | solution.py:200
  279.3 2.0 gather_fusion.1
  281.2 2.3 all-to-all-done.6
  283.6 1.1 subtract_multiply_fusion
  (87 shorter events, 14.7 us)
Async XLA Ops:
  0.6 28.2 %copy-start = (bf16[512,1024]{1,0:T(8,128)(2,1)S(1)}, bf16[512,1024]{1,0:T(8,128)(2,1)}, u32[]{:S(2)}) copy-start(bf16[512,1024]{1,0:T(8,128)(2,1)} %param.11) | copy-start | bytes 3145732
  0.6 28.6 %copy-start.5 = (s32[512]{0:T(512)S(1)}, s32[512]{0:T(512)}, u32[]{:S(2)}) copy-start(s32[512]{0:T(512)} %param.15) | copy-start | bytes 6148
  0.7 28.7 %copy-start.1 = (bf16[256,1024]{1,0:T(8,128)(2,1)S(1)}, bf16[256,1024]{1,0:T(8,128)(2,1)}, u32[]{:S(2)}) copy-start(bf16[256,1024]{1,0:T(8,128)(2,1)} %param.17) | copy-start | bytes 1572868
  0.7 30.0 %copy-start.4 = (s32[16,256]{1,0:T(8,128)S(1)}, s32[16,256]{1,0:T(8,128)}, u32[]{:S(2)}) copy-start(s32[16,256]{1,0:T(8,128)} %param.16) | copy-start | bytes 49156
  0.7 39.4 %collective-permute-start = (bf16[64,2048]{1,0:T(8,128)(2,1)}, bf16[64,2048]{1,0:T(8,128)(2,1)}, u32[]{:S(2)}, u32[]{:S(2)}) collective-permute-start(bf16[64,2048]{1,0:T(8,128)(2,1)} %param.19), channel_id=1, source_target_pairs={{0,1},{1,2},{2,3},{3,4},{4,5},{5,6},{6,7},{7,8},{8,9},{9,10},{10,1... | collective-permute-start | bytes 786440 | tf_op jit(solution)/shard_map/ppermute | solution.py:22
  5.2 38.1 %collective-permute-start.1 = (bf16[64,2048]{1,0:T(8,128)(2,1)}, bf16[64,2048]{1,0:T(8,128)(2,1)}, u32[]{:S(2)}, u32[]{:S(2)}) collective-permute-start(bf16[64,2048]{1,0:T(8,128)(2,1)} %param.19), channel_id=1, source_target_pairs={{0,15},{1,0},{2,1},{3,2},{4,3},{5,4},{6,5},{7,6},{8,7},{9,8},{10,9... | collective-permute-start | bytes 786440 | tf_op jit(solution)/shard_map/ppermute | solution.py:25
  16.6 124.7 %all-to-all-start = ((bf16[16,512,64]{1,2,0:T(8,128)(2,1)}), bf16[16,512,64]{1,2,0:T(8,128)(2,1)}, u32[]{:S(2)}, u32[]{:S(2)}) async-start(bf16[16,512,64]{1,2,0:T(8,128)(2,1)} %broadcast_in_dim.46), calls=%async_computation | async-start | bytes 2097152 | tf_op jit(solution)/shard_map/all_to_all | solution.py:40
  28.8 5.2 %copy-start.2 = (bf16[64,2048]{1,0:T(8,128)(2,1)S(1)}, bf16[64,2048]{1,0:T(8,128)(2,1)}, u32[]{:S(2)}) copy-start(bf16[64,2048]{1,0:T(8,128)(2,1)} %param.19) | copy-start | bytes 786436
  28.8 5.9 %copy-start.3 = (s32[1,32]{1,0:T(1,128)S(1)}, s32[1,32]{1,0:T(1,128)}, u32[]{:S(2)}) copy-start(s32[1,32]{1,0:T(1,128)} %param.12) | copy-start | bytes 388
  28.8 5.9 %copy-start.6 = (s32[1,32]{1,0:T(1,128)S(1)}, s32[1,32]{1,0:T(1,128)}, u32[]{:S(2)}) copy-start(s32[1,32]{1,0:T(1,128)} %param.14) | copy-start | bytes 388
  28.8 5.9 %copy-start.7 = (s32[1,32]{1,0:T(1,128)S(1)}, s32[1,32]{1,0:T(1,128)}, u32[]{:S(2)}) copy-start(s32[1,32]{1,0:T(1,128)} %param.13) | copy-start | bytes 388
  39.2 92.1 %copy-start.8 = (f32[1024]{0:T(1024)S(1)}, f32[1024]{0:T(1024)}, u32[]{:S(2)}) copy-start(f32[1024]{0:T(1024)} %param.18) | copy-start | bytes 12292
  40.1 38.6 %collective-permute-start.2 = (bf16[64,2048]{1,0:T(8,128)(2,1)}, bf16[64,2048]{1,0:T(8,128)(2,1)S(1)}, u32[]{:S(2)}, u32[]{:S(2)}) collective-permute-start(bf16[64,2048]{1,0:T(8,128)(2,1)} %collective-permute-done), channel_id=1, source_target_pairs={{0,1},{1,2},{2,3},{3,4},{4,5},{5,6},{6,7},{7,8},{8,9},{9,10},{10,1... | collective-permute-start | bytes 786440 | tf_op jit(solution)/shard_map/ppermute | solution.py:22
  43.3 37.2 %collective-permute-start.3 = (bf16[64,2048]{1,0:T(8,128)(2,1)}, bf16[64,2048]{1,0:T(8,128)(2,1)S(1)}, u32[]{:S(2)}, u32[]{:S(2)}) collective-permute-start(bf16[64,2048]{1,0:T(8,128)(2,1)} %collective-permute-done.1), channel_id=1, source_target_pairs={{0,15},{1,0},{2,1},{3,2},{4,3},{5,4},{6,5},{7,6},{8,7},{9,8},{10,9... | collective-permute-start | bytes 786440 | tf_op jit(solution)/shard_map/ppermute | solution.py:25
  78.6 9.6 %collective-permute-start.4 = (bf16[64,2048]{1,0:T(8,128)(2,1)S(1)}, bf16[64,2048]{1,0:T(8,128)(2,1)S(1)}, u32[]{:S(2)}, u32[]{:S(2)}) collective-permute-start(bf16[64,2048]{1,0:T(8,128)(2,1)S(1)} %collective-permute-done.2), channel_id=1, source_target_pairs={{0,1},{1,2},{2,3},{3,4},{4,5},{5,6},{6,7},{7,8},{8,9},{9,10},{10,1... | collective-permute-start | bytes 786440 | tf_op jit(solution)/shard_map/ppermute | solution.py:22
  80.6 9.6 %collective-permute-start.5 = (bf16[64,2048]{1,0:T(8,128)(2,1)S(1)}, bf16[64,2048]{1,0:T(8,128)(2,1)S(1)}, u32[]{:S(2)}, u32[]{:S(2)}) collective-permute-start(bf16[64,2048]{1,0:T(8,128)(2,1)S(1)} %collective-permute-done.3), channel_id=1, source_target_pairs={{0,15},{1,0},{2,1},{3,2},{4,3},{5,4},{6,5},{7,6},{8,7},{9,8},{10,9... | collective-permute-start | bytes 786440 | tf_op jit(solution)/shard_map/ppermute | solution.py:25
  88.2 8.7 %collective-permute-start.6 = (bf16[64,2048]{1,0:T(8,128)(2,1)S(1)}, bf16[64,2048]{1,0:T(8,128)(2,1)S(1)}, u32[]{:S(2)}, u32[]{:S(2)}) collective-permute-start(bf16[64,2048]{1,0:T(8,128)(2,1)S(1)} %collective-permute-done.4), channel_id=1, source_target_pairs={{0,1},{1,2},{2,3},{3,4},{4,5},{5,6},{6,7},{7,8},{8,9},{9,10},{10,1... | collective-permute-start | bytes 786440 | tf_op jit(solution)/shard_map/ppermute | solution.py:22
  90.1 8.7 %collective-permute-start.7 = (bf16[64,2048]{1,0:T(8,128)(2,1)S(1)}, bf16[64,2048]{1,0:T(8,128)(2,1)S(1)}, u32[]{:S(2)}, u32[]{:S(2)}) collective-permute-start(bf16[64,2048]{1,0:T(8,128)(2,1)S(1)} %collective-permute-done.5), channel_id=1, source_target_pairs={{0,15},{1,0},{2,1},{3,2},{4,3},{5,4},{6,5},{7,6},{8,7},{9,8},{10,9... | collective-permute-start | bytes 786440 | tf_op jit(solution)/shard_map/ppermute | solution.py:25
  96.9 8.3 %collective-permute-start.8 = (bf16[64,2048]{1,0:T(8,128)(2,1)S(1)}, bf16[64,2048]{1,0:T(8,128)(2,1)S(1)}, u32[]{:S(2)}, u32[]{:S(2)}) collective-permute-start(bf16[64,2048]{1,0:T(8,128)(2,1)S(1)} %collective-permute-done.6), channel_id=1, source_target_pairs={{0,1},{1,2},{2,3},{3,4},{4,5},{5,6},{6,7},{7,8},{8,9},{9,10},{10,1... | collective-permute-start | bytes 786440 | tf_op jit(solution)/shard_map/ppermute | solution.py:22
  98.8 8.3 %collective-permute-start.9 = (bf16[64,2048]{1,0:T(8,128)(2,1)S(1)}, bf16[64,2048]{1,0:T(8,128)(2,1)S(1)}, u32[]{:S(2)}, u32[]{:S(2)}) collective-permute-start(bf16[64,2048]{1,0:T(8,128)(2,1)S(1)} %collective-permute-done.7), channel_id=1, source_target_pairs={{0,15},{1,0},{2,1},{3,2},{4,3},{5,4},{6,5},{7,6},{8,7},{9,8},{10,9... | collective-permute-start | bytes 786440 | tf_op jit(solution)/shard_map/ppermute | solution.py:25
  105.2 8.3 %collective-permute-start.10 = (bf16[64,2048]{1,0:T(8,128)(2,1)S(1)}, bf16[64,2048]{1,0:T(8,128)(2,1)S(1)}, u32[]{:S(2)}, u32[]{:S(2)}) collective-permute-start(bf16[64,2048]{1,0:T(8,128)(2,1)S(1)} %collective-permute-done.8), channel_id=1, source_target_pairs={{0,1},{1,2},{2,3},{3,4},{4,5},{5,6},{6,7},{7,8},{8,9},{9,10},{10,1... | collective-permute-start | bytes 786440 | tf_op jit(solution)/shard_map/ppermute | solution.py:22
  107.2 8.3 %collective-permute-start.11 = (bf16[64,2048]{1,0:T(8,128)(2,1)S(1)}, bf16[64,2048]{1,0:T(8,128)(2,1)S(1)}, u32[]{:S(2)}, u32[]{:S(2)}) collective-permute-start(bf16[64,2048]{1,0:T(8,128)(2,1)S(1)} %collective-permute-done.9), channel_id=1, source_target_pairs={{0,15},{1,0},{2,1},{3,2},{4,3},{5,4},{6,5},{7,6},{8,7},{9,8},{10,9... | collective-permute-start | bytes 786440 | tf_op jit(solution)/shard_map/ppermute | solution.py:25
  113.6 8.3 %collective-permute-start.12 = (bf16[64,2048]{1,0:T(8,128)(2,1)S(1)}, bf16[64,2048]{1,0:T(8,128)(2,1)S(1)}, u32[]{:S(2)}, u32[]{:S(2)}) collective-permute-start(bf16[64,2048]{1,0:T(8,128)(2,1)S(1)} %collective-permute-done.10), channel_id=1, source_target_pairs={{0,1},{1,2},{2,3},{3,4},{4,5},{5,6},{6,7},{7,8},{8,9},{9,10},{10,1... | collective-permute-start | bytes 786440 | tf_op jit(solution)/shard_map/ppermute | solution.py:22
  115.5 9.0 %collective-permute-start.13 = (bf16[64,2048]{1,0:T(8,128)(2,1)S(1)}, bf16[64,2048]{1,0:T(8,128)(2,1)S(1)}, u32[]{:S(2)}, u32[]{:S(2)}) collective-permute-start(bf16[64,2048]{1,0:T(8,128)(2,1)S(1)} %collective-permute-done.11), channel_id=1, source_target_pairs={{0,15},{1,0},{2,1},{3,2},{4,3},{5,4},{6,5},{7,6},{8,7},{9,8},{10,9... | collective-permute-start | bytes 786440 | tf_op jit(solution)/shard_map/ppermute | solution.py:25
  121.9 8.7 %collective-permute-start.14 = (bf16[64,2048]{1,0:T(8,128)(2,1)S(1)}, bf16[64,2048]{1,0:T(8,128)(2,1)S(1)}, u32[]{:S(2)}, u32[]{:S(2)}) collective-permute-start(bf16[64,2048]{1,0:T(8,128)(2,1)S(1)} %collective-permute-done.12), channel_id=1, source_target_pairs={{0,1},{1,2},{2,3},{3,4},{4,5},{5,6},{6,7},{7,8},{8,9},{9,10},{10,1... | collective-permute-start | bytes 786440 | tf_op jit(solution)/shard_map/ppermute | solution.py:22
  141.3 30.9 %all-to-all-start.3 = ((bf16[16,16,1024]{2,1,0:T(8,128)(2,1)}), bf16[16,16,1024]{2,1,0:T(8,128)(2,1)}, u32[]{:S(2)}, u32[]{:S(2)}) async-start(bf16[16,16,1024]{2,1,0:T(8,128)(2,1)} %bitcast.21), calls=%async_computation.3 | async-start | bytes 1048576 | tf_op jit(solution)/shard_map/all_to_all | solution.py:171
  153.2 4.9 %copy-start.9 = (f32[512]{0:T(512)S(1)}, f32[512]{0:T(512)}, u32[]{:S(2)}) copy-start(f32[512]{0:T(512)} %param.20) | copy-start | bytes 6148
  172.2 24.1 %all-to-all-start.2 = ((s32[32,1,2]{2,1,0:T(1,128)}), s32[32,1,2]{2,1,0:T(1,128)S(1)}, u32[]{:S(2)}, u32[]{:S(2)}) async-start(s32[32,1,2]{2,1,0:T(1,128)} %copy.55), calls=%async_computation.2 | async-start | bytes 32768 | tf_op jit(solution)/shard_map/all_to_all | solution.py:114
  191.1 5.3 %copy-start.10 = (f32[512,256]{0,1:T(8,128)}, f32[512,256]{0,1:T(8,128)S(1)}, u32[]{:S(2)}) copy-start(f32[512,256]{0,1:T(8,128)S(1)} %get-tuple-element.42) | copy-start | bytes 1572868
  196.3 29.9 %all-to-all-start.4 = ((bf16[16,16,1024]{2,1,0:T(8,128)(2,1)}), bf16[16,16,1024]{2,1,0:T(8,128)(2,1)S(1)}, u32[]{:S(2)}, u32[]{:S(2)}) async-start(bf16[16,16,1024]{2,1,0:T(8,128)(2,1)} %bitcast.23), calls=%async_computation.4 | async-start | bytes 1048576 | tf_op jit(solution)/shard_map/all_to_all | solution.py:204
  228.2 23.0 %all-to-all-start.5 = ((bf16[32,256,32]{1,2,0:T(8,128)(2,1)}), bf16[32,256,32]{1,2,0:T(8,128)(2,1)}, u32[]{:S(2)}, u32[]{:S(2)}) async-start(bf16[32,256,32]{1,2,0:T(8,128)(2,1)} %bitcast.26), calls=%async_computation.5 | async-start | bytes 1048576 | tf_op jit(solution)/shard_map/all_to_all | solution.py:57
  251.2 20.5 %all-to-all-start.1 = ((bf16[32,16,1024]{2,1,0:T(8,128)(2,1)}), bf16[32,16,1024]{2,1,0:T(8,128)(2,1)S(1)}, u32[]{:S(2)}, u32[]{:S(2)}) async-start(bf16[32,16,1024]{2,1,0:T(8,128)(2,1)} %broadcast_select_fusion), calls=%async_computation.1 | async-start | bytes 2097152 | tf_op jit(solution)/shard_map/all_to_all | solution.py:113
  272.3 11.2 %all-to-all-start.6 = ((f32[32,1,256]{2,1,0:T(1,128)}), f32[32,1,256]{2,1,0:T(1,128)S(1)}, u32[]{:S(2)}, u32[]{:S(2)}) async-start(f32[32,1,256]{2,1,0:T(1,128)} %broadcast_in_dim.55), calls=%async_computation.6 | async-start | bytes 65536 | tf_op jit(solution)/shard_map/all_to_all | solution.py:40
